TPU v7x, 32 devices: a whole 2x2x4 slice. The times are simulated.
32 devices in a mesh: clip: 2 (over x), frame: 8 (over z, y), band: 2 (over core).
Axes of the slice: x: 2, y: 2, z: 4, core: 2. Of those that a mesh axis runs over, the one named last changes fastest.
Arguments:
- pixels: bfloat16 [16, 16, 32, 256], P(('clip', 'frame'), 'band'), parts along dimension 0, may hold values from -40 to 40
- gru_state: bfloat16 [16, 16, 32, 128], P(('clip', 'frame'), 'band'), parts along dimension 0, may hold values from -1 to 1
- tokens: bfloat16 [16, 1024, 256], P(('clip', 'frame'), 'band'), parts along dimension 0, may hold values from -30 to 30
- visible: int32 [16, 1024], P(('clip', 'frame'), 'band'), parts along dimension 0, may hold values from 0 to 1, as said below
- query_frame: int32 [2048], P(('clip', 'band')), parts along dimension 0, may hold values from 0 to 7, as said below
- pixel_query: bfloat16 [256, 256], replicated, may hold values from -2 to 2
- pixel_key: bfloat16 [256, 256], replicated, may hold values from -2 to 2
- pixel_value: bfloat16 [256, 256], replicated, may hold values from -0.375 to 0.375
- pixel_out: bfloat16 [256, 128], replicated, may hold values from -1.5 to 1.5
- time_query: bfloat16 [256, 256], replicated, may hold values from -2 to 2
- time_key: bfloat16 [256, 256], replicated, may hold values from -2 to 2
- time_value: bfloat16 [256, 256], replicated, may hold values from -0.375 to 0.375
- time_out: bfloat16 [256, 256], replicated, may hold values from -0.75 to 0.75
- gru_gates: bfloat16 [3, 3, 256, 256], replicated, may hold values from -0.125 to 0.125
- gru_candidate: bfloat16 [3, 3, 256, 128], replicated, may hold values from -0.125 to 0.125
Outputs:
- refined_state: bfloat16 [16, 16, 32, 128], P(('clip', 'frame'), 'band'), parts along dimension 0
- track_out: bfloat16 [16, 1024, 256], P(('clip', 'frame'), 'band'), parts along dimension 0
There are 2 independent parts, one for each index of `clip`. A program takes and returns all parts, laid end to end along the dimension named above; an argument that names none is the same for every part. Nothing has to cross between parts.
Inputs may be any that keep to these rules, and one draw needn't show every extreme that they name: Each track is visible in the frame named by its query frame index. `query_frame`: every frame is the query frame of exactly 128 tracks.
All inputs are finite; a program needn't handle non-finite values.
Results may differ from a plain program's by a relative error of at most 0.0095.
The roundings to bfloat16 on the way count: a program that leaves them out, or rounds other values in their place, can miss the bound.
Values may be sent and summed in bfloat16 or wider, within the bound.
A program may use at most 64 MiB of HBM per device.

v0:
```python
import jax
import jax.numpy as jnp
from jax import lax
from jax.sharding import PartitionSpec as P

HEADS = 8
HEAD_DIM = 32
GRU_WIDTH = 128
ITERS = 2


def with_halo(x, sides, width):
    for axis, dim in sides:
        devices, length = (lax.axis_size(axis), x.shape[dim])
        up = [(i, (i + 1) % devices) for i in range(devices - 1)]
        down = [(j, i) for i, j in up]
        last = lax.slice_in_dim(x, length - width, length, axis=dim)
        first = lax.slice_in_dim(x, 0, width, axis=dim)
        before = lax.ppermute(last, axis, up)
        after = lax.ppermute(first, axis, down)
        x = jnp.concatenate([before, x, after], axis=dim)
    return x


def attend_heads(queries, key_rows, value_rows, key_mask):
    score_scale = HEAD_DIM ** (-0.5)
    head_outputs = []
    for head_index in range(HEADS):
        offset = head_index * HEAD_DIM
        scores = (
            jnp.dot(
                queries[:, offset : offset + HEAD_DIM],
                key_rows[:, offset : offset + HEAD_DIM].T,
                preferred_element_type=jnp.float32,
            )
            * score_scale
        )
        scores = jnp.where(key_mask[None, :], scores, -jnp.inf)
        weights = jax.nn.softmax(scores, axis=-1).astype(jnp.bfloat16)
        head_outputs.append(
            jnp.dot(
                weights,
                value_rows[:, offset : offset + HEAD_DIM],
                preferred_element_type=jnp.float32,
            )
        )
    return jnp.concatenate(head_outputs, axis=-1).astype(jnp.bfloat16)


def conv_rows(padded, weight, rows, columns):
    widened = jnp.pad(padded, ((0, 0), (1, 1), (0, 0)))
    summed = jnp.zeros((rows * columns, weight.shape[3]), jnp.float32)
    for row_shift in range(3):
        for col_shift in range(3):
            window = widened[row_shift : row_shift + rows, col_shift : col_shift + columns]
            summed = summed + jnp.dot(
                window.reshape(rows * columns, -1),
                weight[row_shift, col_shift],
                preferred_element_type=jnp.float32,
            )
    return summed


def temporal_core(query_part, key_part, value_part, seen_part, anchor_part):
    frames_here, track_count, channels = query_part.shape
    anchor = jnp.einsum("fk,fkc->kc", anchor_part, query_part, preferred_element_type=jnp.float32)
    joint_query = (query_part.astype(jnp.float32) + anchor[None]).astype(jnp.bfloat16)
    shaped = (frames_here, track_count, HEADS, HEAD_DIM)
    scores = jnp.einsum(
        "fkhd,gkhd->khfg",
        joint_query.reshape(shaped),
        key_part.reshape(shaped),
        preferred_element_type=jnp.float32,
    ) * HEAD_DIM ** (-0.5)
    key_mask = jnp.transpose(seen_part) > 0
    scores = jnp.where(key_mask[:, None, None, :], scores, -jnp.inf)
    weights = jax.nn.softmax(scores, axis=-1).astype(jnp.bfloat16)
    attended = jnp.einsum(
        "khfg,gkhd->fkhd", weights, value_part.reshape(shaped), preferred_element_type=jnp.float32
    )
    return attended.astype(jnp.bfloat16).reshape(frames_here, track_count, channels)


def on_device(
    pixels,
    gru_state,
    tokens,
    visible,
    query_frame,
    pixel_query,
    pixel_key,
    pixel_value,
    pixel_out,
    time_query,
    time_key,
    time_value,
    time_out,
    gru_gates,
    gru_candidate,
):
    frame_pos = lax.axis_index("frame")
    frames = lax.axis_size("frame")
    channels = tokens.shape[2]
    half_tracks = tokens.shape[1]
    per_device = half_tracks // frames
    band_rows = pixels.shape[1]
    columns = pixels.shape[2]
    local_tokens = tokens[0]
    seen_mask = visible[0].astype(jnp.bfloat16)
    anchor_mask = (query_frame == frame_pos).astype(jnp.bfloat16)
    seen_split = seen_mask.reshape(1, frames, per_device)
    anchor_split = anchor_mask.reshape(1, frames, per_device)
    token_part = lax.all_to_all(
        local_tokens.reshape(1, frames, per_device, channels),
        "frame",
        split_axis=1,
        concat_axis=0,
        tiled=True,
    )
    seen_part = lax.all_to_all(seen_split, "frame", split_axis=1, concat_axis=0, tiled=True)
    anchor_part = lax.all_to_all(anchor_split, "frame", split_axis=1, concat_axis=0, tiled=True)
    token_rows = token_part[:, 0]
    frames_here, track_count, width_here = token_rows.shape
    flat_rows = token_rows.reshape(frames_here * track_count, width_here)
    outputs = []
    for weight in (time_query, time_key, time_value):
        outputs.append(
            jnp.dot(flat_rows, weight, preferred_element_type=jnp.float32)
            .astype(jnp.bfloat16)
            .reshape(frames_here, track_count, width_here)
        )
    result = temporal_core(outputs[0], outputs[1], outputs[2], seen_part[:, 0], anchor_part[:, 0])
    track_result = result[:, None]
    flat_pixels = pixels[0].reshape(band_rows * columns, channels)
    queries = jnp.dot(flat_pixels, pixel_query, preferred_element_type=jnp.float32).astype(
        jnp.bfloat16
    )
    key_local = jnp.dot(local_tokens, pixel_key, preferred_element_type=jnp.float32).astype(
        jnp.bfloat16
    )
    value_local = jnp.dot(local_tokens, pixel_value, preferred_element_type=jnp.float32).astype(
        jnp.bfloat16
    )
    key_rows, value_rows, seen_all = (
        lax.all_gather(key_local, "band", axis=0, tiled=True),
        lax.all_gather(value_local, "band", axis=0, tiled=True),
        lax.all_gather(seen_mask, "band", axis=0, tiled=True),
    )
    attended = attend_heads(queries, key_rows, value_rows, seen_all > 0)
    context = (
        jnp.dot(attended, pixel_out, preferred_element_type=jnp.float32)
        .astype(jnp.bfloat16)
        .reshape(band_rows, columns, GRU_WIDTH)
    )
    returned = lax.all_to_all(track_result, "frame", split_axis=0, concat_axis=1, tiled=True)
    returned_rows = returned.reshape(half_tracks, channels)
    track_update = jnp.dot(returned_rows, time_out, preferred_element_type=jnp.float32)
    track_out = (local_tokens.astype(jnp.float32) + track_update).astype(jnp.bfloat16)[None]
    state_now = gru_state[0]
    for iteration in range(ITERS):
        combined = jnp.concatenate([state_now, context], axis=-1)
        padded = with_halo(combined, (("band", 0),), 1)
        gate_terms = conv_rows(padded, gru_gates, band_rows, columns)
        update = jax.nn.sigmoid(gate_terms[:, :GRU_WIDTH])
        reset_gate = jax.nn.sigmoid(gate_terms[:, GRU_WIDTH:])
        state_flat = state_now.reshape(band_rows * columns, GRU_WIDTH).astype(jnp.float32)
        reset_state = (
            (reset_gate * state_flat).astype(jnp.bfloat16).reshape(band_rows, columns, GRU_WIDTH)
        )
        mixed_in = jnp.concatenate([reset_state, context], axis=-1)
        padded_mix = with_halo(mixed_in, (("band", 0),), 1)
        candidate = jnp.tanh(conv_rows(padded_mix, gru_candidate, band_rows, columns))
        state_now = (
            ((1.0 - update) * state_flat + update * candidate)
            .astype(jnp.bfloat16)
            .reshape(band_rows, columns, GRU_WIDTH)
        )
    refined_state = state_now[None]
    return (refined_state, track_out)


def solution(mesh):
    placed = (
        P(("clip", "frame"), "band", None, None),
        P(("clip", "frame"), "band", None, None),
        P(("clip", "frame"), "band", None),
        P(("clip", "frame"), "band"),
        P(("clip", "band")),
        P(),
        P(),
        P(),
        P(),
        P(),
        P(),
        P(),
        P(),
        P(),
        P(),
    )
    return jax.shard_map(
        on_device,
        mesh=mesh,
        in_specs=placed,
        out_specs=(P(("clip", "frame"), "band", None, None), P(("clip", "frame"), "band", None)),
        check_vma=False,
    )
```

profile of v0, /device:TPU:0, one launch (start us, length us, event | category | flops | bytes accessed | tf_op | source)
XLA Modules:
  0.0 105.7 jit_solution(6565268605685878097)
XLA Ops:
  2.7 2.3 %all_gather.10 = bf16[1024,256]{1,0:T(8,128)(2,1)S(1)} all-gather(bf16[512,256]{1,0:T(8,128)(2,1)S(1)} %convolution_convert_fusion.5), channel_id=1, replica_groups=mesh['clip'=2,'frame'=8,'band'=2] {'band'}, dimensions={0}, use_global_device_ids=true | all-gather | bytes 786432 | tf_op jit(solution)/shard_map/all_gather | solution.py:145
  5.0 1.9 %all-gather = bf16[1,1024]{1,0:T(2,128)(2,1)S(1)} all-gather(bf16[1,512]{1,0:T(2,128)(2,1)S(1)} %convert_element_type.112), channel_id=2, replica_groups=mesh['clip'=2,'frame'=8,'band'=2] {'band'}, dimensions={1}, use_global_device_ids=true | all-gather | bytes 3072 | tf_op jit(solution)/shard_map/all_gather | solution.py:147
  12.1 2.2 %all_gather.11 = bf16[1024,256]{1,0:T(8,128)(2,1)S(1)} all-gather(bf16[512,256]{1,0:T(8,128)(2,1)S(1)} %convolution_convert_fusion.4), channel_id=1, replica_groups=mesh['clip'=2,'frame'=8,'band'=2] {'band'}, dimensions={0}, use_global_device_ids=true | all-gather | bytes 786432 | tf_op jit(solution)/shard_map/all_gather | solution.py:146
  21.1 2.4 %collective-permute-start = (bf16[1,32,256]{2,1,0:T(8,128)(2,1)S(1)}, bf16[1,32,256]{2,1,0:T(8,128)(2,1)S(1)}, u32[]{:S(2)}, u32[]{:S(2)}) collective-permute-start(bf16[1,32,256]{2,1,0:T(8,128)(2,1)S(1)} %get-tuple-element.42), channel_id=1, source_target_pairs={{0,1},{2,3},{4,5},{6,7},{8,9},{10,11},{12,13},{14,15},{16,17},{18,... | collective-permute-start | bytes 49160 | tf_op jit(solution)/shard_map/ppermute | solution.py:19
  23.5 1.3 %collective-permute-start.1 = (bf16[1,32,256]{2,1,0:T(8,128)(2,1)S(1)}, bf16[1,32,256]{2,1,0:T(8,128)(2,1)S(1)}, u32[]{:S(2)}, u32[]{:S(2)}) collective-permute-start(bf16[1,32,256]{2,1,0:T(8,128)(2,1)S(1)} %get-tuple-element.2), channel_id=1, source_target_pairs={{1,0},{3,2},{5,4},{7,6},{9,8},{11,10},{13,12},{15,14},{17,16},{19,... | collective-permute-start | bytes 49160 | tf_op jit(solution)/shard_map/ppermute | solution.py:20
  25.5 7.0 %all-to-all-start.2 = ((bf16[1,8,64]{2,0,1:T(2,128)(2,1)}), bf16[1,8,64]{2,0,1:T(2,128)(2,1)S(1)}, u32[]{:S(2)}, u32[]{:S(2)}) async-start(bf16[1,8,64]{2,0,1:T(2,128)(2,1)} %reshape.250), calls=%async_computation.2 | async-start | bytes 8192 | tf_op jit(solution)/shard_map/all_to_all | solution.py:121
  34.5 2.7 %collective-permute-start.2 = (bf16[1,32,256]{2,1,0:T(8,128)(2,1)S(1)}, bf16[1,32,256]{2,1,0:T(8,128)(2,1)S(1)}, u32[]{:S(2)}, u32[]{:S(2)}) collective-permute-start(bf16[1,32,256]{2,1,0:T(8,128)(2,1)S(1)} %get-tuple-element.40), channel_id=1, source_target_pairs={{0,1},{2,3},{4,5},{6,7},{8,9},{10,11},{12,13},{14,15},{16,17},{18,... | collective-permute-start | bytes 49160 | tf_op jit(solution)/shard_map/ppermute | solution.py:19
  37.2 1.3 %collective-permute-start.3 = (bf16[1,32,256]{2,1,0:T(8,128)(2,1)S(1)}, bf16[1,32,256]{2,1,0:T(8,128)(2,1)S(1)}, u32[]{:S(2)}, u32[]{:S(2)}) collective-permute-start(bf16[1,32,256]{2,1,0:T(8,128)(2,1)S(1)} %get-tuple-element.41), channel_id=1, source_target_pairs={{1,0},{3,2},{5,4},{7,6},{9,8},{11,10},{13,12},{15,14},{17,16},{19,... | collective-permute-start | bytes 49160 | tf_op jit(solution)/shard_map/ppermute | solution.py:20
  42.1 2.1 %collective-permute-start.4 = (bf16[1,32,256]{2,1,0:T(8,128)(2,1)S(1)}, bf16[1,32,256]{2,1,0:T(8,128)(2,1)S(1)}, u32[]{:S(2)}, u32[]{:S(2)}) collective-permute-start(bf16[1,32,256]{2,1,0:T(8,128)(2,1)S(1)} %get-tuple-element.38), channel_id=1, source_target_pairs={{0,1},{2,3},{4,5},{6,7},{8,9},{10,11},{12,13},{14,15},{16,17},{18,... | collective-permute-start | bytes 49160 | tf_op jit(solution)/shard_map/ppermute | solution.py:19
  44.2 1.3 %collective-permute-start.5 = (bf16[1,32,256]{2,1,0:T(8,128)(2,1)S(1)}, bf16[1,32,256]{2,1,0:T(8,128)(2,1)S(1)}, u32[]{:S(2)}, u32[]{:S(2)}) collective-permute-start(bf16[1,32,256]{2,1,0:T(8,128)(2,1)S(1)} %get-tuple-element.39), channel_id=1, source_target_pairs={{1,0},{3,2},{5,4},{7,6},{9,8},{11,10},{13,12},{15,14},{17,16},{19,... | collective-permute-start | bytes 49160 | tf_op jit(solution)/shard_map/ppermute | solution.py:20
  45.5 5.7 %all-to-all-start.1 = ((bf16[1,8,64]{2,0,1:T(2,128)(2,1)}), bf16[1,8,64]{2,0,1:T(2,128)(2,1)S(1)}, u32[]{:S(2)}, u32[]{:S(2)}) async-start(bf16[1,8,64]{2,0,1:T(2,128)(2,1)} %convert_element_type.145), calls=%async_computation.1 | async-start | bytes 8192 | tf_op jit(solution)/shard_map/all_to_all | solution.py:120
  53.9 2.7 %collective-permute-start.6 = (bf16[1,32,256]{2,1,0:T(8,128)(2,1)S(1)}, bf16[1,32,256]{2,1,0:T(8,128)(2,1)S(1)}, u32[]{:S(2)}, u32[]{:S(2)}) collective-permute-start(bf16[1,32,256]{2,1,0:T(8,128)(2,1)S(1)} %get-tuple-element.36), channel_id=1, source_target_pairs={{0,1},{2,3},{4,5},{6,7},{8,9},{10,11},{12,13},{14,15},{16,17},{18,... | collective-permute-start | bytes 49160 | tf_op jit(solution)/shard_map/ppermute | solution.py:19
  56.6 1.3 %collective-permute-start.7 = (bf16[1,32,256]{2,1,0:T(8,128)(2,1)S(1)}, bf16[1,32,256]{2,1,0:T(8,128)(2,1)S(1)}, u32[]{:S(2)}, u32[]{:S(2)}) collective-permute-start(bf16[1,32,256]{2,1,0:T(8,128)(2,1)S(1)} %get-tuple-element.37), channel_id=1, source_target_pairs={{1,0},{3,2},{5,4},{7,6},{9,8},{11,10},{13,12},{15,14},{17,16},{19,... | collective-permute-start | bytes 49160 | tf_op jit(solution)/shard_map/ppermute | solution.py:20
  58.0 5.7 %all-to-all-start = ((bf16[1,8,64,256]{3,2,0,1:T(8,128)(2,1)}), bf16[1,8,64,256]{3,2,0,1:T(8,128)(2,1)S(1)}, u32[]{:S(2)}, u32[]{:S(2)}) async-start(bf16[1,8,64,256]{3,2,0,1:T(8,128)(2,1)} %bitcast.61), calls=%async_computation | async-start | bytes 524288 | tf_op jit(solution)/shard_map/all_to_all | solution.py:113
  67.1 6.8 %all-to-all-done = bf16[1,8,64,256]{3,2,0,1:T(8,128)(2,1)S(1)} async-done(((bf16[1,8,64,256]{3,2,0,1:T(8,128)(2,1)}), bf16[1,8,64,256]{3,2,0,1:T(8,128)(2,1)S(1)}, u32[]{:S(2)}, u32[]{:S(2)}) %all-to-all-start) | async-done | bytes 262176 | tf_op jit(solution)/shard_map/all_to_all | solution.py:113
  74.8 1.8 %copy.70 = bf16[8,64,8,32]{3,0,2,1:T(8,128)(2,1)S(1)} copy(bf16[8,64,8,32]{1,0,3,2:T(8,128)(2,1)S(1)} %add_convert_fusion) | data formatting | bytes 524288 | tf_op jit(solution)/shard_map/convert_element_type | solution.py:67
  77.2 2.7 %copy.71 = bf16[8,64,8,32]{3,0,2,1:T(8,128)(2,1)} copy(bf16[8,64,8,32]{1,0,3,2:T(8,128)(2,1)S(1)} %reshape_reshape.7) | data formatting | bytes 524288 | tf_op jit(solution)/shard_map/reshape;reshape | solution.py:72
  79.9 1.9 %fusion.205 = f32[64,8,8,8]{2,3,1,0:T(8,128)S(1)} fusion(bf16[8,64,8,32]{3,0,2,1:T(8,128)(2,1)S(1)} %copy.70, bf16[8,64,8,32]{3,0,2,1:T(8,128)(2,1)} %copy.71), kind=kOutput, calls=%fused_computation.340 | convolution fusion | flops 2097152 | bytes 655360 | tf_op jit(solution)/shard_map/fkhd,gkhd->khfg/dot_general | solution.py:69
  84.2 1.6 %copy.74 = bf16[64,8,8,8]{3,2,1,0:T(8,128)(2,1)S(1)} copy(bf16[64,8,8,8]{0,3,2,1:T(8,128)(2,1)S(1)} %divide_convert_fusion.16) | data formatting | bytes 131072 | tf_op jit(solution)/shard_map/convert_element_type | solution.py:77
  86.5 1.8 %copy.73 = bf16[8,64,8,32]{3,0,2,1:T(8,128)(2,1)S(1)} copy(bf16[8,64,8,32]{1,0,3,2:T(8,128)(2,1)S(1)} %reshape_reshape.6) | data formatting | bytes 524288 | tf_op jit(solution)/shard_map/reshape;reshape | solution.py:79
  91.0 3.6 %all-to-all-start.3 = ((bf16[8,1,64,256]{3,2,1,0:T(8,128)(2,1)}), bf16[8,1,64,256]{3,2,1,0:T(8,128)(2,1)S(1)}, u32[]{:S(2)}, u32[]{:S(2)}) async-start(bf16[8,1,64,256]{3,2,1,0:T(8,128)(2,1)} %copy.76), calls=%async_computation.3 | async-start | bytes 524288 | tf_op jit(solution)/shard_map/all_to_all | solution.py:155
  95.7 1.7 %fusion.24 = bf16[256,128]{1,0:T(8,128)(2,1)} fusion(f32[256,128]{1,0:T(8,128)S(1)} %fusion.138, f32[256,128]{1,0:T(8,128)S(1)} %copy-done.16, bf16[256,256]{1,0:T(8,128)(2,1)S(1)} %bitcast.277, bf16[256,128]{1,0:T(8,128)(2,1)S(1)} %copy-done.5, f32[256,256]{1,0:T(8,128)S(1)} %copy-done.7, bf16[3,3,256,128]{3,2,1,0:T(8,128)(2,1)} %param.29), kind=kOutput, calls=%fused_computation.68 | convolution fusion | flops 17137664 | bytes 720896 | tf_op jit(solution)/shard_map/dot_general | solution.py:56
  97.4 6.5 %all-to-all-done.3 = bf16[8,1,64,256]{3,2,1,0:T(8,128)(2,1)S(1)} async-done(((bf16[8,1,64,256]{3,2,1,0:T(8,128)(2,1)}), bf16[8,1,64,256]{3,2,1,0:T(8,128)(2,1)S(1)}, u32[]{:S(2)}, u32[]{:S(2)}) %all-to-all-start.3) | async-done | bytes 262176 | tf_op jit(solution)/shard_map/all_to_all | solution.py:155
  103.9 1.9 %fusion.12 = bf16[1,512,256]{2,1,0:T(8,128)(2,1)} fusion(bf16[512,256]{1,0:T(8,128)(2,1)S(1)} %bitcast.244, bf16[256,256]{1,0:T(8,128)(2,1)S(1)} %copy-done.15, bf16[1,512,256]{2,1,0:T(8,128)(2,1)} %param.17), kind=kOutput, calls=%fused_computation.27 | convolution fusion | flops 67502080 | bytes 917504 | tf_op jit(solution)/shard_map/dot_general | solution.py:157
  (159 shorter events, 34.1 us)
Async XLA Ops:
  0.7 6.3 %copy-start.9 = (bf16[1,8,32,256]{3,2,1,0:T(8,128)(2,1)S(1)}, bf16[1,8,32,256]{3,2,1,0:T(8,128)(2,1)}, u32[]{:S(2)}) copy-start(bf16[1,8,32,256]{3,2,1,0:T(8,128)(2,1)} %param.15) | copy-start | bytes 393220
  0.7 6.3 %copy-start.10 = (bf16[256,256]{1,0:T(8,128)(2,1)S(1)}, bf16[256,256]{1,0:T(8,128)(2,1)}, u32[]{:S(2)}) copy-start(bf16[256,256]{1,0:T(8,128)(2,1)} %param.20) | copy-start | bytes 393220
  20.8 11.8 %copy-start.1 = (bf16[3,3,256,256]{3,2,1,0:T(8,128)(2,1)S(1)}, bf16[3,3,256,256]{3,2,1,0:T(8,128)(2,1)}, u32[]{:S(2)}) copy-start(bf16[3,3,256,256]{3,2,1,0:T(8,128)(2,1)} %param.28) | copy-start | bytes 3538948
  21.1 11.4 %collective-permute-start = (bf16[1,32,256]{2,1,0:T(8,128)(2,1)S(1)}, bf16[1,32,256]{2,1,0:T(8,128)(2,1)S(1)}, u32[]{:S(2)}, u32[]{:S(2)}) collective-permute-start(bf16[1,32,256]{2,1,0:T(8,128)(2,1)S(1)} %get-tuple-element.42), channel_id=1, source_target_pairs={{0,1},{2,3},{4,5},{6,7},{8,9},{10,11},{12,13},{14,15},{16,17},{18,... | collective-permute-start | bytes 49160 | tf_op jit(solution)/shard_map/ppermute | solution.py:19
  23.5 9.0 %collective-permute-start.1 = (bf16[1,32,256]{2,1,0:T(8,128)(2,1)S(1)}, bf16[1,32,256]{2,1,0:T(8,128)(2,1)S(1)}, u32[]{:S(2)}, u32[]{:S(2)}) collective-permute-start(bf16[1,32,256]{2,1,0:T(8,128)(2,1)S(1)} %get-tuple-element.2), channel_id=1, source_target_pairs={{1,0},{3,2},{5,4},{7,6},{9,8},{11,10},{13,12},{15,14},{17,16},{19,... | collective-permute-start | bytes 49160 | tf_op jit(solution)/shard_map/ppermute | solution.py:20
  25.5 20.0 %all-to-all-start.2 = ((bf16[1,8,64]{2,0,1:T(2,128)(2,1)}), bf16[1,8,64]{2,0,1:T(2,128)(2,1)S(1)}, u32[]{:S(2)}, u32[]{:S(2)}) async-start(bf16[1,8,64]{2,0,1:T(2,128)(2,1)} %reshape.250), calls=%async_computation.2 | async-start | bytes 8192 | tf_op jit(solution)/shard_map/all_to_all | solution.py:121
  34.2 6.3 %copy-start.2 = (bf16[3,3,256,128]{3,2,1,0:T(8,128)(2,1)S(1)}, bf16[3,3,256,128]{3,2,1,0:T(8,128)(2,1)}, u32[]{:S(2)}) copy-start(bf16[3,3,256,128]{3,2,1,0:T(8,128)(2,1)} %param.29) | copy-start | bytes 1769476
  34.5 4.8 %collective-permute-start.2 = (bf16[1,32,256]{2,1,0:T(8,128)(2,1)S(1)}, bf16[1,32,256]{2,1,0:T(8,128)(2,1)S(1)}, u32[]{:S(2)}, u32[]{:S(2)}) collective-permute-start(bf16[1,32,256]{2,1,0:T(8,128)(2,1)S(1)} %get-tuple-element.40), channel_id=1, source_target_pairs={{0,1},{2,3},{4,5},{6,7},{8,9},{10,11},{12,13},{14,15},{16,17},{18,... | collective-permute-start | bytes 49160 | tf_op jit(solution)/shard_map/ppermute | solution.py:19
  37.2 3.1 %collective-permute-start.3 = (bf16[1,32,256]{2,1,0:T(8,128)(2,1)S(1)}, bf16[1,32,256]{2,1,0:T(8,128)(2,1)S(1)}, u32[]{:S(2)}, u32[]{:S(2)}) collective-permute-start(bf16[1,32,256]{2,1,0:T(8,128)(2,1)S(1)} %get-tuple-element.41), channel_id=1, source_target_pairs={{1,0},{3,2},{5,4},{7,6},{9,8},{11,10},{13,12},{15,14},{17,16},{19,... | collective-permute-start | bytes 49160 | tf_op jit(solution)/shard_map/ppermute | solution.py:20
  42.1 11.1 %copy-start.4 = (bf16[256,128]{1,0:T(8,128)(2,1)}, bf16[256,128]{1,0:T(8,128)(2,1)S(1)}, u32[]{:S(2)}) copy-start(bf16[256,128]{1,0:T(8,128)(2,1)S(1)} %fusion.25) | copy-start | bytes 196612
  42.1 9.1 %collective-permute-start.4 = (bf16[1,32,256]{2,1,0:T(8,128)(2,1)S(1)}, bf16[1,32,256]{2,1,0:T(8,128)(2,1)S(1)}, u32[]{:S(2)}, u32[]{:S(2)}) collective-permute-start(bf16[1,32,256]{2,1,0:T(8,128)(2,1)S(1)} %get-tuple-element.38), channel_id=1, source_target_pairs={{0,1},{2,3},{4,5},{6,7},{8,9},{10,11},{12,13},{14,15},{16,17},{18,... | collective-permute-start | bytes 49160 | tf_op jit(solution)/shard_map/ppermute | solution.py:19
  44.2 7.0 %collective-permute-start.5 = (bf16[1,32,256]{2,1,0:T(8,128)(2,1)S(1)}, bf16[1,32,256]{2,1,0:T(8,128)(2,1)S(1)}, u32[]{:S(2)}, u32[]{:S(2)}) collective-permute-start(bf16[1,32,256]{2,1,0:T(8,128)(2,1)S(1)} %get-tuple-element.39), channel_id=1, source_target_pairs={{1,0},{3,2},{5,4},{7,6},{9,8},{11,10},{13,12},{15,14},{17,16},{19,... | collective-permute-start | bytes 49160 | tf_op jit(solution)/shard_map/ppermute | solution.py:20
  45.5 12.4 %all-to-all-start.1 = ((bf16[1,8,64]{2,0,1:T(2,128)(2,1)}), bf16[1,8,64]{2,0,1:T(2,128)(2,1)S(1)}, u32[]{:S(2)}, u32[]{:S(2)}) async-start(bf16[1,8,64]{2,0,1:T(2,128)(2,1)} %convert_element_type.145), calls=%async_computation.1 | async-start | bytes 8192 | tf_op jit(solution)/shard_map/all_to_all | solution.py:120
  53.9 9.8 %collective-permute-start.6 = (bf16[1,32,256]{2,1,0:T(8,128)(2,1)S(1)}, bf16[1,32,256]{2,1,0:T(8,128)(2,1)S(1)}, u32[]{:S(2)}, u32[]{:S(2)}) collective-permute-start(bf16[1,32,256]{2,1,0:T(8,128)(2,1)S(1)} %get-tuple-element.36), channel_id=1, source_target_pairs={{0,1},{2,3},{4,5},{6,7},{8,9},{10,11},{12,13},{14,15},{16,17},{18,... | collective-permute-start | bytes 49160 | tf_op jit(solution)/shard_map/ppermute | solution.py:19
  56.6 7.1 %collective-permute-start.7 = (bf16[1,32,256]{2,1,0:T(8,128)(2,1)S(1)}, bf16[1,32,256]{2,1,0:T(8,128)(2,1)S(1)}, u32[]{:S(2)}, u32[]{:S(2)}) collective-permute-start(bf16[1,32,256]{2,1,0:T(8,128)(2,1)S(1)} %get-tuple-element.37), channel_id=1, source_target_pairs={{1,0},{3,2},{5,4},{7,6},{9,8},{11,10},{13,12},{15,14},{17,16},{19,... | collective-permute-start | bytes 49160 | tf_op jit(solution)/shard_map/ppermute | solution.py:20
  58.0 15.9 %all-to-all-start = ((bf16[1,8,64,256]{3,2,0,1:T(8,128)(2,1)}), bf16[1,8,64,256]{3,2,0,1:T(8,128)(2,1)S(1)}, u32[]{:S(2)}, u32[]{:S(2)}) async-start(bf16[1,8,64,256]{3,2,0,1:T(8,128)(2,1)} %bitcast.61), calls=%async_computation | async-start | bytes 524288 | tf_op jit(solution)/shard_map/all_to_all | solution.py:113
  65.5 8.3 %copy-start.12 = (bf16[256,256]{1,0:T(8,128)(2,1)S(1)}, bf16[256,256]{1,0:T(8,128)(2,1)}, u32[]{:S(2)}) copy-start(bf16[256,256]{1,0:T(8,128)(2,1)} %param.24) | copy-start | bytes 393220
  88.9 5.8 %copy-start.8 = (bf16[8,32,256]{2,1,0:T(8,128)(2,1)S(1)}, bf16[8,32,256]{2,1,0:T(8,128)(2,1)}, u32[]{:S(2)}) copy-start(bf16[8,32,256]{2,1,0:T(8,128)(2,1)} %get-tuple-element.8) | copy-start | bytes 393220
  90.1 5.6 %copy-start.5 = (bf16[256,128]{1,0:T(8,128)(2,1)S(1)}, bf16[256,128]{1,0:T(8,128)(2,1)}, u32[]{:S(2)}) copy-start(bf16[256,128]{1,0:T(8,128)(2,1)} %copy-done.4) | copy-start | bytes 196612
  90.1 5.6 %copy-start.7 = (f32[256,256]{1,0:T(8,128)S(1)}, f32[256,256]{1,0:T(8,128)}, u32[]{:S(2)}) copy-start(f32[256,256]{1,0:T(8,128)} %copy-done.6) | copy-start | bytes 786436
  90.1 5.6 %copy-start.16 = (f32[256,128]{1,0:T(8,128)S(1)}, f32[256,128]{1,0:T(8,128)}, u32[]{:S(2)}) copy-start(f32[256,128]{1,0:T(8,128)} %convolution_add_fusion.16) | copy-start | bytes 393220
  90.1 5.6 %copy-start.17 = (bf16[8,32,256]{2,1,0:T(8,128)(2,1)S(1)}, bf16[8,32,256]{2,1,0:T(8,128)(2,1)}, u32[]{:S(2)}) copy-start(bf16[8,32,256]{2,1,0:T(8,128)(2,1)} %get-tuple-element.28) | copy-start | bytes 393220
  90.1 13.7 %copy-start.15 = (bf16[256,256]{1,0:T(8,128)(2,1)S(1)}, bf16[256,256]{1,0:T(8,128)(2,1)}, u32[]{:S(2)}) copy-start(bf16[256,256]{1,0:T(8,128)(2,1)} %param.27) | copy-start | bytes 393220
  91.0 12.8 %all-to-all-start.3 = ((bf16[8,1,64,256]{3,2,1,0:T(8,128)(2,1)}), bf16[8,1,64,256]{3,2,1,0:T(8,128)(2,1)S(1)}, u32[]{:S(2)}, u32[]{:S(2)}) async-start(bf16[8,1,64,256]{3,2,1,0:T(8,128)(2,1)} %copy.76), calls=%async_computation.3 | async-start | bytes 524288 | tf_op jit(solution)/shard_map/all_to_all | solution.py:155
  (9 other events, 18.2 us)
where the time goes:
time: 107 us; the launch traced here: 106 us
  starting transfers between devices  37.2 us (35%)
  matrix products  24.6 us (23%)
  local copies, waits for them, and re-layouts  16.6 us (16%)
  waiting for transfers between devices  14.3 us (13%)
  blocking collectives  6.35 us (6%)
  other arithmetic  5.05 us (5%)
  between operations  1.63 us (2%)
    ppermute x4, starting transfers between devices, with_halo(): before = lax.ppermute(last, axis, up)  9.94 us
    dot_general x36, matrix products, conv_rows(): jnp.dot(window.reshape(rows * columns, -1), weight[row_shift, col_shift],...  9.4 us
    all_to_all x1, starting transfers between devices, on_device(): lax.all_to_all(anchor_split, 'frame', split_axis=1, concat_axis=0, tiled=...  6.98 us
    all_to_all x1, waiting for transfers between devices, on_device(): lax.all_to_all(local_tokens.reshape(1, frames, per_device, channels), 'fr...  6.77 us
    all_to_all x1, waiting for transfers between devices, on_device(): lax.all_to_all(track_result, 'frame', split_axis=0, concat_axis=1, tiled=...  6.47 us
    all_to_all x1, starting transfers between devices, on_device(): lax.all_to_all(local_tokens.reshape(1, frames, per_device, channels), 'fr...  5.72 us
    all_to_all x1, starting transfers between devices, on_device(): lax.all_to_all(seen_split, 'frame', split_axis=1, concat_axis=0, tiled=True)  5.72 us
    ppermute x4, starting transfers between devices, with_halo(): after = lax.ppermute(first, axis, down)  5.17 us
  transfers between devices with their start and end apart: 12, of which 3 were waited for; matrix products, arithmetic and copies ran while one was open for 12% of the time, Pallas kernels for 0%

commit v1 on v0

--- a/solution.py
+++ b/solution.py
@@ -7,6 +7,17 @@
 HEAD_DIM = 32
 GRU_WIDTH = 128
 ITERS = 2
+
+
+def in_blocks(x, dim, length):
+    before, after = (x.shape[:dim], x.shape[dim + 1 :])
+    return jnp.moveaxis(x.reshape(*before, length, -1, *after), dim, 0)
+
+
+def in_order(pieces, dim):
+    pieces = jnp.moveaxis(pieces, 0, dim)
+    lengths = pieces.shape
+    return pieces.reshape(*lengths[:dim], lengths[dim] * lengths[dim + 1], *lengths[dim + 2 :])
 
 
 def with_halo(x, sides, width):
@@ -117,7 +128,14 @@
         concat_axis=0,
         tiled=True,
     )
-    seen_part = lax.all_to_all(seen_split, "frame", split_axis=1, concat_axis=0, tiled=True)
+    count, index = (lax.axis_size("frame"), lax.axis_index("frame"))
+    pieces = in_blocks(seen_split, 1, count)
+    done = [pieces[index]]
+    for step in range(1, count):
+        sent = pieces[index ^ step]
+        done.append(lax.ppermute(sent, "frame", [(i_2, i_2 ^ step) for i_2 in range(count)]))
+    pieces = jnp.stack(done)[index ^ jnp.arange(count)]
+    seen_part = in_order(pieces, 0)
     anchor_part = lax.all_to_all(anchor_split, "frame", split_axis=1, concat_axis=0, tiled=True)
     token_rows = token_part[:, 0]
     frames_here, track_count, width_here = token_rows.shape

time: 107 us -> 118 us (1.10)
  waiting for transfers between devices: 14.3 us -> 21.2 us
  starting transfers between devices: 37.2 us -> 40.3 us
  other arithmetic: 5.05 us -> 7.19 us
    ppermute x0 -> x7, starting transfers between devices: none -> 13.9 us  [on_device(): lax.ppermute(sent, 'frame', [(i_2, i_2 ^ step) for i_2 in range(count)])]
    all_to_all x1 -> x0, starting transfers between devices: 5.72 us -> none  [on_device(): lax.all_to_all(seen_split, 'frame', split_axis=1, concat_axis=0, tiled=True)]
    ppermute x0 -> x7, waiting for transfers between devices: none -> 4.74 us  [on_device(): lax.ppermute(sent, 'frame', [(i_2, i_2 ^ step) for i_2 in range(count)])]
    ppermute x4, waiting for transfers between devices: 1.08 us -> 3.51 us  [with_halo(): after = lax.ppermute(first, axis, down)]
    ppermute x4, starting transfers between devices: 9.94 us -> 7.62 us  [with_halo(): before = lax.ppermute(last, axis, up)]
    all_to_all x1, starting transfers between devices: 5.72 us -> 3.61 us  [on_device(): lax.all_to_all(local_tokens.reshape(1, frames, per_device, channels), 'fr...]
    convert_element_type x2, other arithmetic: 0.03 us -> 1.47 us  [on_device(): seen_mask = visible[0].astype(jnp.bfloat16)]
  transfers between devices with their start and end apart: 12 -> 18, of which waited for: 3 -> 6; matrix products, arithmetic and copies ran while one was open for 12% -> 23% of each run, Pallas kernels for 0% -> 0%
where the time goes in v1:
time: 118 us; the launch traced here: 117 us
  starting transfers between devices  40.3 us (34%)
  matrix products  24.6 us (21%)
  waiting for transfers between devices  21.2 us (18%)
  local copies, waits for them, and re-layouts  15.8 us (13%)
  other arithmetic  7.19 us (6%)
  blocking collectives  6.19 us (5%)
  between operations  1.66 us (1%)
    ppermute x7, starting transfers between devices, on_device(): lax.ppermute(sent, 'frame', [(i_2, i_2 ^ step) for i_2 in range(count)])  13.9 us
    dot_general x36, matrix products, conv_rows(): jnp.dot(window.reshape(rows * columns, -1), weight[row_shift, col_shift],...  9.39 us
    ppermute x4, starting transfers between devices, with_halo(): before = lax.ppermute(last, axis, up)  7.62 us
    all_to_all x1, waiting for transfers between devices, on_device(): lax.all_to_all(track_result, 'frame', split_axis=0, concat_axis=1, tiled=...  6.48 us
    all_to_all x1, waiting for transfers between devices, on_device(): lax.all_to_all(local_tokens.reshape(1, frames, per_device, channels), 'fr...  6.47 us
    all_to_all x1, starting transfers between devices, on_device(): lax.all_to_all(anchor_split, 'frame', split_axis=1, concat_axis=0, tiled=...  6.22 us
    ppermute x4, starting transfers between devices, with_halo(): after = lax.ppermute(first, axis, down)  5.17 us
    ppermute x7, waiting for transfers between devices, on_device(): lax.ppermute(sent, 'frame', [(i_2, i_2 ^ step) for i_2 in range(count)])  4.74 us
  transfers between devices with their start and end apart: 18, of which 6 were waited for; matrix products, arithmetic and copies ran while one was open for 23% of the time, Pallas kernels for 0%

profile of v1, /device:TPU:0, one launch (start us, length us, event | category | flops | bytes accessed | tf_op | source)
XLA Modules:
  0.0 116.9 jit_solution(17420221626987052189)
XLA Ops:
  1.6 3.1 %collective-permute-start.8 = (bf16[1,1,64]{2,1,0:T(2,128)(2,1)S(1)}, bf16[1,1,64]{2,1,0:T(2,128)(2,1)S(1)}, u32[]{:S(2)}, u32[]{:S(2)}) collective-permute-start(bf16[1,1,64]{2,1,0:T(2,128)(2,1)S(1)} %get-tuple-element.49), channel_id=1, source_target_pairs={{0,2},{2,0},{4,6},{6,4},{8,10},{10,8},{12,14},{14,12},{1,3},{3,1},... | collective-permute-start | bytes 392 | tf_op jit(solution)/shard_map/ppermute | solution.py:136
  4.7 1.6 %collective-permute-start.9 = (bf16[1,1,64]{2,1,0:T(2,128)(2,1)S(1)}, bf16[1,1,64]{2,1,0:T(2,128)(2,1)S(1)}, u32[]{:S(2)}, u32[]{:S(2)}) collective-permute-start(bf16[1,1,64]{2,1,0:T(2,128)(2,1)S(1)} %get-tuple-element.48), channel_id=1, source_target_pairs={{0,4},{2,6},{4,0},{6,2},{8,12},{10,14},{12,8},{14,10},{1,5},{3,7},... | collective-permute-start | bytes 392 | tf_op jit(solution)/shard_map/ppermute | solution.py:136
  7.6 6.2 %all-to-all-start.1 = ((bf16[1,8,64]{2,0,1:T(2,128)(2,1)}), bf16[1,8,64]{2,0,1:T(2,128)(2,1)S(1)}, u32[]{:S(2)}, u32[]{:S(2)}) async-start(bf16[1,8,64]{2,0,1:T(2,128)(2,1)} %reshape.280), calls=%async_computation.1 | async-start | bytes 8192 | tf_op jit(solution)/shard_map/all_to_all | solution.py:139
  15.7 2.2 %all_gather.10 = bf16[1024,256]{1,0:T(8,128)(2,1)S(1)} all-gather(bf16[512,256]{1,0:T(8,128)(2,1)S(1)} %convolution_convert_fusion.5), channel_id=1, replica_groups=mesh['clip'=2,'frame'=8,'band'=2] {'band'}, dimensions={0}, use_global_device_ids=true | all-gather | bytes 786432 | tf_op jit(solution)/shard_map/all_gather | solution.py:163
  17.9 1.8 %all-gather = bf16[1,1024]{1,0:T(2,128)(2,1)S(1)} all-gather(bf16[1,512]{1,0:T(2,128)(2,1)S(1)} %convert_element_type.112), channel_id=2, replica_groups=mesh['clip'=2,'frame'=8,'band'=2] {'band'}, dimensions={1}, use_global_device_ids=true | all-gather | bytes 3072 | tf_op jit(solution)/shard_map/all_gather | solution.py:165
  24.9 2.2 %all_gather.11 = bf16[1024,256]{1,0:T(8,128)(2,1)S(1)} all-gather(bf16[512,256]{1,0:T(8,128)(2,1)S(1)} %convolution_convert_fusion.4), channel_id=1, replica_groups=mesh['clip'=2,'frame'=8,'band'=2] {'band'}, dimensions={0}, use_global_device_ids=true | all-gather | bytes 786432 | tf_op jit(solution)/shard_map/all_gather | solution.py:164
  33.9 2.2 %collective-permute-start = (bf16[1,32,256]{2,1,0:T(8,128)(2,1)S(1)}, bf16[1,32,256]{2,1,0:T(8,128)(2,1)S(1)}, u32[]{:S(2)}, u32[]{:S(2)}) collective-permute-start(bf16[1,32,256]{2,1,0:T(8,128)(2,1)S(1)} %get-tuple-element.42), channel_id=1, source_target_pairs={{0,1},{2,3},{4,5},{6,7},{8,9},{10,11},{12,13},{14,15},{16,17},{18,... | collective-permute-start | bytes 49160 | tf_op jit(solution)/shard_map/ppermute | solution.py:30
  37.4 1.8 %collective-permute-done.1 = bf16[1,32,256]{2,1,0:T(8,128)(2,1)S(1)} collective-permute-done((bf16[1,32,256]{2,1,0:T(8,128)(2,1)S(1)}, bf16[1,32,256]{2,1,0:T(8,128)(2,1)S(1)}, u32[]{:S(2)}, u32[]{:S(2)}) %collective-permute-start.1) | collective-permute-done | bytes 16416 | tf_op jit(solution)/shard_map/ppermute | solution.py:31
  41.2 2.1 %collective-permute-start.2 = (bf16[1,32,256]{2,1,0:T(8,128)(2,1)S(1)}, bf16[1,32,256]{2,1,0:T(8,128)(2,1)S(1)}, u32[]{:S(2)}, u32[]{:S(2)}) collective-permute-start(bf16[1,32,256]{2,1,0:T(8,128)(2,1)S(1)} %get-tuple-element.40), channel_id=1, source_target_pairs={{0,1},{2,3},{4,5},{6,7},{8,9},{10,11},{12,13},{14,15},{16,17},{18,... | collective-permute-start | bytes 49160 | tf_op jit(solution)/shard_map/ppermute | solution.py:30
  44.6 3.0 %collective-permute-start.11 = (bf16[1,1,64]{2,1,0:T(2,128)(2,1)S(1)}, bf16[1,1,64]{2,1,0:T(2,128)(2,1)S(1)}, u32[]{:S(2)}, u32[]{:S(2)}) collective-permute-start(bf16[1,1,64]{2,1,0:T(2,128)(2,1)S(1)} %get-tuple-element.46), channel_id=1, source_target_pairs={{0,8},{2,10},{4,12},{6,14},{8,0},{10,2},{12,4},{14,6},{1,9},{3,11}... | collective-permute-start | bytes 392 | tf_op jit(solution)/shard_map/ppermute | solution.py:136
  49.0 3.3 %collective-permute-start.13 = (bf16[1,1,64]{2,1,0:T(2,128)(2,1)S(1)}, bf16[1,1,64]{2,1,0:T(2,128)(2,1)S(1)}, u32[]{:S(2)}, u32[]{:S(2)}) collective-permute-start(bf16[1,1,64]{2,1,0:T(2,128)(2,1)S(1)} %get-tuple-element.44), channel_id=1, source_target_pairs={{0,12},{2,14},{4,8},{6,10},{8,4},{10,6},{12,0},{14,2},{1,13},{3,15... | collective-permute-start | bytes 392 | tf_op jit(solution)/shard_map/ppermute | solution.py:136
  54.4 4.2 %collective-permute-done.14 = bf16[1,1,64]{2,1,0:T(2,128)(2,1)S(1)} collective-permute-done((bf16[1,1,64]{2,1,0:T(2,128)(2,1)S(1)}, bf16[1,1,64]{2,1,0:T(2,128)(2,1)S(1)}, u32[]{:S(2)}, u32[]{:S(2)}) %collective-permute-start.14) | collective-permute-done | bytes 160 | tf_op jit(solution)/shard_map/ppermute | solution.py:136
  63.6 1.8 %collective-permute-done.5 = bf16[1,32,256]{2,1,0:T(8,128)(2,1)S(1)} collective-permute-done((bf16[1,32,256]{2,1,0:T(8,128)(2,1)S(1)}, bf16[1,32,256]{2,1,0:T(8,128)(2,1)S(1)}, u32[]{:S(2)}, u32[]{:S(2)}) %collective-permute-start.5) | collective-permute-done | bytes 16416 | tf_op jit(solution)/shard_map/ppermute | solution.py:31
  68.0 2.1 %collective-permute-start.6 = (bf16[1,32,256]{2,1,0:T(8,128)(2,1)S(1)}, bf16[1,32,256]{2,1,0:T(8,128)(2,1)S(1)}, u32[]{:S(2)}, u32[]{:S(2)}) collective-permute-start(bf16[1,32,256]{2,1,0:T(8,128)(2,1)S(1)} %get-tuple-element.36), channel_id=1, source_target_pairs={{0,1},{2,3},{4,5},{6,7},{8,9},{10,11},{12,13},{14,15},{16,17},{18,... | collective-permute-start | bytes 49160 | tf_op jit(solution)/shard_map/ppermute | solution.py:30
  71.4 3.6 %all-to-all-start = ((bf16[1,8,64,256]{3,2,0,1:T(8,128)(2,1)}), bf16[1,8,64,256]{3,2,0,1:T(8,128)(2,1)S(1)}, u32[]{:S(2)}, u32[]{:S(2)}) async-start(bf16[1,8,64,256]{3,2,0,1:T(8,128)(2,1)} %bitcast.61), calls=%async_computation | async-start | bytes 524288 | tf_op jit(solution)/shard_map/all_to_all | solution.py:124
  78.4 6.5 %all-to-all-done = bf16[1,8,64,256]{3,2,0,1:T(8,128)(2,1)S(1)} async-done(((bf16[1,8,64,256]{3,2,0,1:T(8,128)(2,1)}), bf16[1,8,64,256]{3,2,0,1:T(8,128)(2,1)S(1)}, u32[]{:S(2)}, u32[]{:S(2)}) %all-to-all-start) | async-done | bytes 262176 | tf_op jit(solution)/shard_map/all_to_all | solution.py:124
  85.8 1.8 %copy.108 = bf16[8,64,8,32]{3,0,2,1:T(8,128)(2,1)S(1)} copy(bf16[8,64,8,32]{1,0,3,2:T(8,128)(2,1)S(1)} %add_convert_fusion) | data formatting | bytes 524288 | tf_op jit(solution)/shard_map/convert_element_type | solution.py:78
  88.3 2.7 %copy.109 = bf16[8,64,8,32]{3,0,2,1:T(8,128)(2,1)} copy(bf16[8,64,8,32]{1,0,3,2:T(8,128)(2,1)S(1)} %reshape_reshape.7) | data formatting | bytes 524288 | tf_op jit(solution)/shard_map/reshape;reshape | solution.py:83
  91.0 1.9 %fusion.213 = f32[64,8,8,8]{2,3,1,0:T(8,128)S(1)} fusion(bf16[8,64,8,32]{3,0,2,1:T(8,128)(2,1)S(1)} %copy.108, bf16[8,64,8,32]{3,0,2,1:T(8,128)(2,1)} %copy.109), kind=kOutput, calls=%fused_computation.359 | convolution fusion | flops 2097152 | bytes 655360 | tf_op jit(solution)/shard_map/fkhd,gkhd->khfg/dot_general | solution.py:80
  97.5 1.8 %copy.111 = bf16[8,64,8,32]{3,0,2,1:T(8,128)(2,1)S(1)} copy(bf16[8,64,8,32]{1,0,3,2:T(8,128)(2,1)S(1)} %reshape_reshape.6) | data formatting | bytes 524288 | tf_op jit(solution)/shard_map/reshape;reshape | solution.py:90
  102.1 3.8 %all-to-all-start.2 = ((bf16[8,1,64,256]{3,2,1,0:T(8,128)(2,1)}), bf16[8,1,64,256]{3,2,1,0:T(8,128)(2,1)S(1)}, u32[]{:S(2)}, u32[]{:S(2)}) async-start(bf16[8,1,64,256]{3,2,1,0:T(8,128)(2,1)} %copy.114), calls=%async_computation.2 | async-start | bytes 524288 | tf_op jit(solution)/shard_map/all_to_all | solution.py:173
  106.9 1.7 %fusion.24 = bf16[256,128]{1,0:T(8,128)(2,1)} fusion(f32[256,128]{1,0:T(8,128)S(1)} %fusion.138, f32[256,128]{1,0:T(8,128)S(1)} %copy-done.16, bf16[256,256]{1,0:T(8,128)(2,1)S(1)} %bitcast.314, bf16[256,128]{1,0:T(8,128)(2,1)S(1)} %copy-done.5, f32[256,256]{1,0:T(8,128)S(1)} %copy-done.7, bf16[3,3,256,128]{3,2,1,0:T(8,128)(2,1)} %param.29), kind=kOutput, calls=%fused_computation.69 | convolution fusion | flops 17137664 | bytes 720896 | tf_op jit(solution)/shard_map/dot_general | solution.py:67
  108.6 6.5 %all-to-all-done.2 = bf16[8,1,64,256]{3,2,1,0:T(8,128)(2,1)S(1)} async-done(((bf16[8,1,64,256]{3,2,1,0:T(8,128)(2,1)}), bf16[8,1,64,256]{3,2,1,0:T(8,128)(2,1)S(1)}, u32[]{:S(2)}, u32[]{:S(2)}) %all-to-all-start.2) | async-done | bytes 262176 | tf_op jit(solution)/shard_map/all_to_all | solution.py:173
  115.0 1.9 %fusion.12 = bf16[1,512,256]{2,1,0:T(8,128)(2,1)} fusion(bf16[512,256]{1,0:T(8,128)(2,1)S(1)} %bitcast.280, bf16[256,256]{1,0:T(8,128)(2,1)S(1)} %copy-done.15, bf16[1,512,256]{2,1,0:T(8,128)(2,1)} %param.17), kind=kOutput, calls=%fused_computation.28 | convolution fusion | flops 67502080 | bytes 917504 | tf_op jit(solution)/shard_map/dot_general | solution.py:175
  (172 shorter events, 45.9 us)
Async XLA Ops:
  0.6 13.9 %copy-start = (bf16[256,256]{1,0:T(8,128)(2,1)S(1)}, bf16[256,256]{1,0:T(8,128)(2,1)}, u32[]{:S(2)}) copy-start(bf16[256,256]{1,0:T(8,128)(2,1)} %param.21) | copy-start | bytes 393220
  0.6 19.1 %copy-start.9 = (bf16[1,8,32,256]{3,2,1,0:T(8,128)(2,1)S(1)}, bf16[1,8,32,256]{3,2,1,0:T(8,128)(2,1)}, u32[]{:S(2)}) copy-start(bf16[1,8,32,256]{3,2,1,0:T(8,128)(2,1)} %param.15) | copy-start | bytes 393220
  0.7 19.1 %copy-start.10 = (bf16[256,256]{1,0:T(8,128)(2,1)S(1)}, bf16[256,256]{1,0:T(8,128)(2,1)}, u32[]{:S(2)}) copy-start(bf16[256,256]{1,0:T(8,128)(2,1)} %param.20) | copy-start | bytes 393220
  1.6 43.0 %collective-permute-start.8 = (bf16[1,1,64]{2,1,0:T(2,128)(2,1)S(1)}, bf16[1,1,64]{2,1,0:T(2,128)(2,1)S(1)}, u32[]{:S(2)}, u32[]{:S(2)}) collective-permute-start(bf16[1,1,64]{2,1,0:T(2,128)(2,1)S(1)} %get-tuple-element.49), channel_id=1, source_target_pairs={{0,2},{2,0},{4,6},{6,4},{8,10},{10,8},{12,14},{14,12},{1,3},{3,1},... | collective-permute-start | bytes 392 | tf_op jit(solution)/shard_map/ppermute | solution.py:136
  4.7 42.9 %collective-permute-start.9 = (bf16[1,1,64]{2,1,0:T(2,128)(2,1)S(1)}, bf16[1,1,64]{2,1,0:T(2,128)(2,1)S(1)}, u32[]{:S(2)}, u32[]{:S(2)}) collective-permute-start(bf16[1,1,64]{2,1,0:T(2,128)(2,1)S(1)} %get-tuple-element.48), channel_id=1, source_target_pairs={{0,4},{2,6},{4,0},{6,2},{8,12},{10,14},{12,8},{14,10},{1,5},{3,7},... | collective-permute-start | bytes 392 | tf_op jit(solution)/shard_map/ppermute | solution.py:136
  6.2 42.8 %collective-permute-start.10 = (bf16[1,1,64]{2,1,0:T(2,128)(2,1)S(1)}, bf16[1,1,64]{2,1,0:T(2,128)(2,1)S(1)}, u32[]{:S(2)}, u32[]{:S(2)}) collective-permute-start(bf16[1,1,64]{2,1,0:T(2,128)(2,1)S(1)} %get-tuple-element.47), channel_id=1, source_target_pairs={{0,6},{2,4},{4,2},{6,0},{8,14},{10,12},{12,10},{14,8},{1,7},{3,5},... | collective-permute-start | bytes 392 | tf_op jit(solution)/shard_map/ppermute | solution.py:136
  7.6 63.8 %all-to-all-start.1 = ((bf16[1,8,64]{2,0,1:T(2,128)(2,1)}), bf16[1,8,64]{2,0,1:T(2,128)(2,1)S(1)}, u32[]{:S(2)}, u32[]{:S(2)}) async-start(bf16[1,8,64]{2,0,1:T(2,128)(2,1)} %reshape.280), calls=%async_computation.1 | async-start | bytes 8192 | tf_op jit(solution)/shard_map/all_to_all | solution.py:139
  33.9 3.5 %collective-permute-start = (bf16[1,32,256]{2,1,0:T(8,128)(2,1)S(1)}, bf16[1,32,256]{2,1,0:T(8,128)(2,1)S(1)}, u32[]{:S(2)}, u32[]{:S(2)}) collective-permute-start(bf16[1,32,256]{2,1,0:T(8,128)(2,1)S(1)} %get-tuple-element.42), channel_id=1, source_target_pairs={{0,1},{2,3},{4,5},{6,7},{8,9},{10,11},{12,13},{14,15},{16,17},{18,... | collective-permute-start | bytes 49160 | tf_op jit(solution)/shard_map/ppermute | solution.py:30
  36.1 3.1 %collective-permute-start.1 = (bf16[1,32,256]{2,1,0:T(8,128)(2,1)S(1)}, bf16[1,32,256]{2,1,0:T(8,128)(2,1)S(1)}, u32[]{:S(2)}, u32[]{:S(2)}) collective-permute-start(bf16[1,32,256]{2,1,0:T(8,128)(2,1)S(1)} %get-tuple-element.2), channel_id=1, source_target_pairs={{1,0},{3,2},{5,4},{7,6},{9,8},{11,10},{13,12},{15,14},{17,16},{19,... | collective-permute-start | bytes 49160 | tf_op jit(solution)/shard_map/ppermute | solution.py:31
  40.9 18.4 %copy-start.2 = (bf16[3,3,256,128]{3,2,1,0:T(8,128)(2,1)S(1)}, bf16[3,3,256,128]{3,2,1,0:T(8,128)(2,1)}, u32[]{:S(2)}) copy-start(bf16[3,3,256,128]{3,2,1,0:T(8,128)(2,1)} %param.29) | copy-start | bytes 1769476
  41.2 18.0 %collective-permute-start.2 = (bf16[1,32,256]{2,1,0:T(8,128)(2,1)S(1)}, bf16[1,32,256]{2,1,0:T(8,128)(2,1)S(1)}, u32[]{:S(2)}, u32[]{:S(2)}) collective-permute-start(bf16[1,32,256]{2,1,0:T(8,128)(2,1)S(1)} %get-tuple-element.40), channel_id=1, source_target_pairs={{0,1},{2,3},{4,5},{6,7},{8,9},{10,11},{12,13},{14,15},{16,17},{18,... | collective-permute-start | bytes 49160 | tf_op jit(solution)/shard_map/ppermute | solution.py:30
  43.2 15.9 %collective-permute-start.3 = (bf16[1,32,256]{2,1,0:T(8,128)(2,1)S(1)}, bf16[1,32,256]{2,1,0:T(8,128)(2,1)S(1)}, u32[]{:S(2)}, u32[]{:S(2)}) collective-permute-start(bf16[1,32,256]{2,1,0:T(8,128)(2,1)S(1)} %get-tuple-element.41), channel_id=1, source_target_pairs={{1,0},{3,2},{5,4},{7,6},{9,8},{11,10},{13,12},{15,14},{17,16},{19,... | collective-permute-start | bytes 49160 | tf_op jit(solution)/shard_map/ppermute | solution.py:31
  44.6 7.7 %collective-permute-start.11 = (bf16[1,1,64]{2,1,0:T(2,128)(2,1)S(1)}, bf16[1,1,64]{2,1,0:T(2,128)(2,1)S(1)}, u32[]{:S(2)}, u32[]{:S(2)}) collective-permute-start(bf16[1,1,64]{2,1,0:T(2,128)(2,1)S(1)} %get-tuple-element.46), channel_id=1, source_target_pairs={{0,8},{2,10},{4,12},{6,14},{8,0},{10,2},{12,4},{14,6},{1,9},{3,11}... | collective-permute-start | bytes 392 | tf_op jit(solution)/shard_map/ppermute | solution.py:136
  47.5 6.3 %collective-permute-start.12 = (bf16[1,1,64]{2,1,0:T(2,128)(2,1)S(1)}, bf16[1,1,64]{2,1,0:T(2,128)(2,1)S(1)}, u32[]{:S(2)}, u32[]{:S(2)}) collective-permute-start(bf16[1,1,64]{2,1,0:T(2,128)(2,1)S(1)} %get-tuple-element.45), channel_id=1, source_target_pairs={{0,10},{2,8},{4,14},{6,12},{8,2},{10,0},{12,6},{14,4},{1,11},{3,9}... | collective-permute-start | bytes 392 | tf_op jit(solution)/shard_map/ppermute | solution.py:136
  49.0 5.4 %collective-permute-start.13 = (bf16[1,1,64]{2,1,0:T(2,128)(2,1)S(1)}, bf16[1,1,64]{2,1,0:T(2,128)(2,1)S(1)}, u32[]{:S(2)}, u32[]{:S(2)}) collective-permute-start(bf16[1,1,64]{2,1,0:T(2,128)(2,1)S(1)} %get-tuple-element.44), channel_id=1, source_target_pairs={{0,12},{2,14},{4,8},{6,10},{8,4},{10,6},{12,0},{14,2},{1,13},{3,15... | collective-permute-start | bytes 392 | tf_op jit(solution)/shard_map/ppermute | solution.py:136
  52.3 6.3 %collective-permute-start.14 = (bf16[1,1,64]{2,1,0:T(2,128)(2,1)S(1)}, bf16[1,1,64]{2,1,0:T(2,128)(2,1)S(1)}, u32[]{:S(2)}, u32[]{:S(2)}) collective-permute-start(bf16[1,1,64]{2,1,0:T(2,128)(2,1)S(1)} %get-tuple-element.43), channel_id=1, source_target_pairs={{0,14},{2,12},{4,10},{6,8},{8,6},{10,4},{12,2},{14,0},{1,15},{3,13... | collective-permute-start | bytes 392 | tf_op jit(solution)/shard_map/ppermute | solution.py:136
  61.0 2.6 %collective-permute-start.4 = (bf16[1,32,256]{2,1,0:T(8,128)(2,1)S(1)}, bf16[1,32,256]{2,1,0:T(8,128)(2,1)S(1)}, u32[]{:S(2)}, u32[]{:S(2)}) collective-permute-start(bf16[1,32,256]{2,1,0:T(8,128)(2,1)S(1)} %get-tuple-element.38), channel_id=1, source_target_pairs={{0,1},{2,3},{4,5},{6,7},{8,9},{10,11},{12,13},{14,15},{16,17},{18,... | collective-permute-start | bytes 49160 | tf_op jit(solution)/shard_map/ppermute | solution.py:30
  62.3 3.1 %collective-permute-start.5 = (bf16[1,32,256]{2,1,0:T(8,128)(2,1)S(1)}, bf16[1,32,256]{2,1,0:T(8,128)(2,1)S(1)}, u32[]{:S(2)}, u32[]{:S(2)}) collective-permute-start(bf16[1,32,256]{2,1,0:T(8,128)(2,1)S(1)} %get-tuple-element.39), channel_id=1, source_target_pairs={{1,0},{3,2},{5,4},{7,6},{9,8},{11,10},{13,12},{15,14},{17,16},{19,... | collective-permute-start | bytes 49160 | tf_op jit(solution)/shard_map/ppermute | solution.py:31
  68.0 7.0 %collective-permute-start.6 = (bf16[1,32,256]{2,1,0:T(8,128)(2,1)S(1)}, bf16[1,32,256]{2,1,0:T(8,128)(2,1)S(1)}, u32[]{:S(2)}, u32[]{:S(2)}) collective-permute-start(bf16[1,32,256]{2,1,0:T(8,128)(2,1)S(1)} %get-tuple-element.36), channel_id=1, source_target_pairs={{0,1},{2,3},{4,5},{6,7},{8,9},{10,11},{12,13},{14,15},{16,17},{18,... | collective-permute-start | bytes 49160 | tf_op jit(solution)/shard_map/ppermute | solution.py:30
  70.1 4.9 %collective-permute-start.7 = (bf16[1,32,256]{2,1,0:T(8,128)(2,1)S(1)}, bf16[1,32,256]{2,1,0:T(8,128)(2,1)S(1)}, u32[]{:S(2)}, u32[]{:S(2)}) collective-permute-start(bf16[1,32,256]{2,1,0:T(8,128)(2,1)S(1)} %get-tuple-element.37), channel_id=1, source_target_pairs={{1,0},{3,2},{5,4},{7,6},{9,8},{11,10},{13,12},{15,14},{17,16},{19,... | collective-permute-start | bytes 49160 | tf_op jit(solution)/shard_map/ppermute | solution.py:31
  71.4 13.5 %all-to-all-start = ((bf16[1,8,64,256]{3,2,0,1:T(8,128)(2,1)}), bf16[1,8,64,256]{3,2,0,1:T(8,128)(2,1)S(1)}, u32[]{:S(2)}, u32[]{:S(2)}) async-start(bf16[1,8,64,256]{3,2,0,1:T(8,128)(2,1)} %bitcast.61), calls=%async_computation | async-start | bytes 524288 | tf_op jit(solution)/shard_map/all_to_all | solution.py:124
  76.9 8.0 %copy-start.12 = (bf16[256,256]{1,0:T(8,128)(2,1)S(1)}, bf16[256,256]{1,0:T(8,128)(2,1)}, u32[]{:S(2)}) copy-start(bf16[256,256]{1,0:T(8,128)(2,1)} %param.24) | copy-start | bytes 393220
  101.2 13.9 %copy-start.15 = (bf16[256,256]{1,0:T(8,128)(2,1)S(1)}, bf16[256,256]{1,0:T(8,128)(2,1)}, u32[]{:S(2)}) copy-start(bf16[256,256]{1,0:T(8,128)(2,1)} %param.27) | copy-start | bytes 393220
  102.1 13.0 %all-to-all-start.2 = ((bf16[8,1,64,256]{3,2,1,0:T(8,128)(2,1)}), bf16[8,1,64,256]{3,2,1,0:T(8,128)(2,1)S(1)}, u32[]{:S(2)}, u32[]{:S(2)}) async-start(bf16[8,1,64,256]{3,2,1,0:T(8,128)(2,1)} %copy.114), calls=%async_computation.2 | async-start | bytes 524288 | tf_op jit(solution)/shard_map/all_to_all | solution.py:173
  (13 other events, 49.1 us)
